TPU v7x, 128 devices: a whole 4x4x4 slice. The times are simulated.
128 devices in a mesh: basis: 16 (over x, z_lo, core), orb: 8 (over z_hi, y).
Axes of the slice: x: 4, y: 4, z: 4 (z_hi: 2, z_lo: 2; z = z_hi * 2 + z_lo), core: 2. Of those that a mesh axis runs over, the one named last changes fastest.
Arguments:
- cont_orbitals: bfloat16 [65536, 2048], P('basis', 'orb'), may hold values from -6 to 6
- target_orbitals: bfloat16 [65536, 1024], P('basis'), may hold values from -0.09375 to 0.09375
- margin_blocks: bfloat16 [256, 4, 256, 256], P('basis'), may hold values from -0.1875 to 0.1875
- dipole_blocks: bfloat16 [256, 4, 256, 256], P('basis'), may hold values from -0.1875 to 0.1875
- band_offsets: int32 [256, 4], P('basis'), may hold values from -2 to 2, as said below
Outputs:
- cont_orth: bfloat16 [65536, 2048], P('basis', 'orb')
- dipole_mo: bfloat16 [1024, 2048], P('basis', 'orb')
Inputs may be any that keep to these rules, and one draw needn't show every extreme that they name: `band_offsets`: each block row names 4 different offsets.
All inputs are finite; a program needn't handle non-finite values.
Results may differ from a plain program's by a relative error of at most 0.012.
Values may be sent and summed in bfloat16 or wider, within the bound.
A program may use at most 128 MiB of HBM per device.

v0:
```python
import jax
import jax.numpy as jnp
from jax import lax
from jax.sharding import PartitionSpec as P

BK = 256
KB = 4


def padded_2(block, sides, width):
    for axis, dim in sides:
        count = lax.axis_size(axis)
        forward = [(i, i + 1) for i in range(count - 1)]
        backward = [(target, source) for source, target in forward]
        low = lax.ppermute(
            lax.slice_in_dim(block, block.shape[dim] - width, None, axis=dim), axis, forward
        )
        high = lax.ppermute(lax.slice_in_dim(block, 0, width, axis=dim), axis, backward)
        block = jnp.concatenate([low, block, high], axis=dim)
    return block


def band_local(blocks, offsets, padded):
    nblk = blocks.shape[0]
    width = padded.shape[1]
    stacked = padded.reshape(nblk + 4, BK, width)
    total = jnp.zeros((nblk, BK, width), jnp.float32)
    for k in range(KB):
        index = jnp.arange(nblk, dtype=jnp.int32) + 2 + offsets[:, k]
        taken = stacked[index]
        total = total + jnp.einsum(
            "bij,bjc->bic", blocks[:, k], taken, preferred_element_type=jnp.float32
        )
    return total.reshape(nblk * BK, width)


def on_device(cont_orbitals, target_orbitals, margin_blocks, dipole_blocks, band_offsets):
    cont_padded = padded_2(cont_orbitals, (("basis", 0),), 2 * BK)
    margin_cont = band_local(margin_blocks, band_offsets, cont_padded).astype(jnp.bfloat16)
    partial_proj = lax.dot_general(
        target_orbitals, margin_cont, (((0,), (0,)), ((), ())), preferred_element_type=jnp.float32
    )
    projection = lax.psum(partial_proj, "basis")
    projection_b = projection.astype(jnp.bfloat16)
    removed = jnp.dot(target_orbitals, projection_b, preferred_element_type=jnp.float32)
    cont_orth = (cont_orbitals.astype(jnp.float32) - removed).astype(jnp.bfloat16)
    squares = jnp.sum(jnp.square(cont_orth.astype(jnp.float32)), axis=0)
    orth_padded = padded_2(cont_orth, (("basis", 0),), 2 * BK)
    total_squares = lax.psum(squares, "basis")
    col_norm = 1.0 / jnp.sqrt(
        total_squares / (band_offsets.shape[0] * BK * lax.axis_size("basis")) + 1e-06
    )
    dipole_cont = band_local(dipole_blocks, band_offsets, orth_padded).astype(jnp.bfloat16)
    dipole_raw = lax.psum_scatter(
        lax.dot_general(
            target_orbitals,
            dipole_cont,
            (((0,), (0,)), ((), ())),
            preferred_element_type=jnp.float32,
        ),
        "basis",
        scatter_dimension=0,
        tiled=True,
    )
    dipole_mo = (dipole_raw * col_norm[None, :]).astype(jnp.bfloat16)
    return (cont_orth, dipole_mo)


def solution(mesh):
    return jax.shard_map(
        on_device,
        mesh=mesh,
        in_specs=(
            P("basis", "orb"),
            P("basis", None),
            P("basis", None, None, None),
            P("basis", None, None, None),
            P("basis", None),
        ),
        out_specs=(P("basis", "orb"), P("basis", "orb")),
        check_vma=False,
    )
```

profile of v0, /device:TPU:0, one launch (start us, length us, event | category | flops | bytes accessed | tf_op | source)
XLA Modules:
  0.0 222.3 jit_solution(11804426336611701205)
XLA Ops:
  8.3 1.3 collective-permute-start
  11.7 4.1 %copy.30 = bf16[4096,256]{0,1:T(8,128)(2,1)} copy(bf16[4096,256]{1,0:T(8,128)(2,1)} %param.5) | data formatting | bytes 4194304 | tf_op args[0]
  15.9 1.8 pad_maximum_fusion
  17.6 2.0 gather_fusion.3
  19.6 2.0 gather_fusion.2
  21.6 2.0 gather_fusion.1
  23.7 2.0 gather_fusion
  25.7 3.1 %fusion.10 = f32[16,256,256]{1,2,0:T(8,128)S(1)} fusion(bf16[16,256,256]{2,1,0:T(8,128)(2,1)} %gather_fusion.2, bf16[16,4,256,256]{3,2,1,0:T(8,128)(2,1)} %param.7), kind=kOutput, calls=%fused_computation.24 | convolution fusion | flops 536870912 | bytes 8388608 | tf_op jit(solution)/shard_map/bij,bjc->bic/dot_general | solution.py:31
  28.8 2.5 %fusion.14 = f32[16,256,256]{1,2,0:T(8,128)S(1)} fusion(bf16[16,256,256]{2,1,0:T(8,128)(2,1)S(1)} %copy-done.7, bf16[16,4,256,256]{3,2,1,0:T(8,128)(2,1)} %param.7), kind=kOutput, calls=%fused_computation.28 | convolution fusion | flops 536870912 | bytes 8388608 | tf_op jit(solution)/shard_map/bij,bjc->bic/dot_general | solution.py:31
  31.3 2.5 %fusion.12 = f32[16,256,256]{1,2,0:T(8,128)S(1)} fusion(bf16[16,256,256]{2,1,0:T(8,128)(2,1)S(1)} %copy-done.5, bf16[16,4,256,256]{3,2,1,0:T(8,128)(2,1)} %param.7), kind=kOutput, calls=%fused_computation.26 | convolution fusion | flops 536870912 | bytes 8388608 | tf_op jit(solution)/shard_map/bij,bjc->bic/dot_general | solution.py:31
  33.8 3.0 %add_convert_fusion.1 = bf16[16,256,256]{1,2,0:T(8,128)(2,1)S(1)} fusion(f32[16,256,256]{1,2,0:T(8,128)S(1)} %fusion.10, f32[16,256,256]{1,2,0:T(8,128)S(1)} %fusion.14, f32[16,256,256]{1,2,0:T(8,128)S(1)} %fusion.12, bf16[16,256,256]{2,1,0:T(8,128)(2,1)S(1)} %copy-done.3, bf16[16,4,256,256]{3,2,1,0:T(8,128)(2,1)} %param.7), kind=kOutput, calls=%fused_computation.13 | convolution fusion | flops 541065216 | bytes 18874368 | tf_op jit(solution)/shard_map/bij,bjc->bic/dot_general | solution.py:31
  36.9 2.3 %convolution_bitcast_fusion.2 = f32[1024,256]{0,1:T(8,128)S(1)} fusion(bf16[4096,256]{1,0:T(8,128)(2,1)S(1)} %bitcast.93, bf16[4096,1024]{1,0:T(8,128)(2,1)S(1)} %bitcast.82), kind=kOutput, calls=%fused_computation.39 | convolution fusion | flops 2147483648 | bytes 11534336 | tf_op jit(solution)/shard_map/dot_general | solution.py:40
  39.2 70.3 %all-reduce.1 = bf16[1024,256]{0,1:T(8,128)(2,1)} all-reduce(f32[1024,256]{0,1:T(8,128)S(1)} %convolution_bitcast_fusion.2), channel_id=1, replica_groups=mesh['basis'=16,'orb'=8] {'basis'}, use_global_device_ids=true, to_apply=%region_0.0 | all-reduce | flops 262144 | bytes 1572864 | tf_op jit(solution)/shard_map/psum | solution.py:43
  109.6 6.2 %multiply_reduce_fusion = (f32[256]{0:T(256)S(1)}, bf16[4096,256]{0,1:T(8,128)(2,1)S(1)}) fusion(bf16[1024,256]{0,1:T(8,128)(2,1)} %all-reduce.1, bf16[4096,1024]{1,0:T(8,128)(2,1)} %param.6, bf16[4096,256]{0,1:T(8,128)(2,1)S(1)} %copy-done.8), kind=kOutput, calls=%fused_computation.11 | convolution fusion | flops 2153774848 | bytes 13108224 | tf_op jit(solution)/shard_map/dot_general | solution.py:45
  115.8 1.3 collective-permute-start.2
  117.2 1.5 collective-permute-start.3
  118.6 1.9 collective-permute-done.3
  120.6 1.7 pad_maximum_fusion.1
  122.3 3.0 %copy.35 = bf16[5120,256]{1,0:T(8,128)(2,1)S(1)} copy(bf16[5120,256]{0,1:T(8,128)(2,1)} %pad_maximum_fusion.1) | data formatting | bytes 5242880 | tf_op jit(solution)/shard_map/concatenate | solution.py:19
  125.3 2.0 gather_fusion.7
  127.3 2.0 gather_fusion.6
  129.3 2.0 gather_fusion.5
  131.4 2.0 gather_fusion.4
  133.4 3.1 %fusion.7 = f32[16,256,256]{1,2,0:T(8,128)S(1)} fusion(bf16[16,256,256]{2,1,0:T(8,128)(2,1)} %gather_fusion.4, bf16[16,4,256,256]{3,2,1,0:T(8,128)(2,1)} %param.8), kind=kOutput, calls=%fused_computation.21 | convolution fusion | flops 536870912 | bytes 8388608 | tf_op jit(solution)/shard_map/bij,bjc->bic/dot_general | solution.py:31
  136.5 2.5 %fusion.5 = f32[16,256,256]{1,2,0:T(8,128)S(1)} fusion(bf16[16,256,256]{2,1,0:T(8,128)(2,1)S(1)} %copy-done.6, bf16[16,4,256,256]{3,2,1,0:T(8,128)(2,1)} %param.8), kind=kOutput, calls=%fused_computation.19 | convolution fusion | flops 536870912 | bytes 8388608 | tf_op jit(solution)/shard_map/bij,bjc->bic/dot_general | solution.py:31
  139.0 2.5 %fusion.3 = f32[16,256,256]{1,2,0:T(8,128)S(1)} fusion(bf16[16,256,256]{2,1,0:T(8,128)(2,1)S(1)} %copy-done.4, bf16[16,4,256,256]{3,2,1,0:T(8,128)(2,1)} %param.8), kind=kOutput, calls=%fused_computation.17 | convolution fusion | flops 536870912 | bytes 8388608 | tf_op jit(solution)/shard_map/bij,bjc->bic/dot_general | solution.py:31
  141.5 3.0 %add_convert_fusion = bf16[16,256,256]{1,2,0:T(8,128)(2,1)S(1)} fusion(f32[16,256,256]{1,2,0:T(8,128)S(1)} %fusion.3, f32[16,256,256]{1,2,0:T(8,128)S(1)} %fusion.7, f32[16,256,256]{1,2,0:T(8,128)S(1)} %fusion.5, bf16[16,256,256]{2,1,0:T(8,128)(2,1)S(1)} %copy-done.2, bf16[16,4,256,256]{3,2,1,0:T(8,128)(2,1)} %param.8), kind=kOutput, calls=%fused_computation.12 | convolution fusion | flops 541065216 | bytes 18874368 | tf_op jit(solution)/shard_map/bij,bjc->bic/dot_general | solution.py:31
  144.6 2.3 %convolution_bitcast_fusion.1 = f32[1024,256]{0,1:T(8,128)S(1)} fusion(bf16[4096,256]{1,0:T(8,128)(2,1)S(1)} %bitcast.94, bf16[4096,1024]{1,0:T(8,128)(2,1)S(1)} %bitcast.84), kind=kOutput, calls=%fused_computation.38 | convolution fusion | flops 2147483648 | bytes 11534336 | tf_op jit(solution)/shard_map/dot_general | solution.py:55
  146.9 1.3 copy.42
  148.9 2.4 %copy.40 = bf16[4096,256]{1,0:T(8,128)(2,1)} copy(bf16[4096,256]{0,1:T(8,128)(2,1)S(1)} %copy-done.1) | data formatting | bytes 4194304
  151.3 29.2 %psum.15 = f32[256]{0:T(256)S(1)} all-reduce(f32[256]{0:T(256)S(1)} %get-tuple-element.16), channel_id=1, replica_groups=mesh['basis'=16,'orb'=8] {'basis'}, use_global_device_ids=true, to_apply=%region_3.0 | all-reduce | flops 256 | bytes 2048 | tf_op jit(solution)/shard_map/psum | solution.py:49
  180.5 33.2 %reduce-scatter.4.cloned.1.call-done = f32[64,256]{1,0:T(8,128)} async-done(((f32[1024,256]{1,0:T(8,128)}), f32[64,256]{1,0:T(8,128)}) %reduce-scatter.4.cloned.1.call-update) | async-done | bytes 65552
  (43 shorter events, 5.9 us)
Async XLA Ops:
  7.2 206.6 %reduce-scatter.4.cloned.1.call-start = ((), (), s32[]{:S(2)}) async-start(), calls=%async_computation.1 | async-start | bytes 1114112
  8.3 7.6 %collective-permute-start = (bf16[512,256]{1,0:T(8,128)(2,1)S(1)}, bf16[512,256]{1,0:T(8,128)(2,1)S(1)}, u32[]{:S(2)}, u32[]{:S(2)}) collective-permute-start(bf16[512,256]{1,0:T(8,128)(2,1)S(1)} %get-tuple-element.10), channel_id=1, source_target_pairs={{0,8},{8,16},{16,24},{24,32},{32,40},{40,48},{48,56},{56,64},{64,7... | collective-permute-start | bytes 786440 | tf_op jit(solution)/shard_map/ppermute | solution.py:15
  9.6 6.3 %collective-permute-start.1 = (bf16[512,256]{1,0:T(8,128)(2,1)S(1)}, bf16[512,256]{1,0:T(8,128)(2,1)S(1)}, u32[]{:S(2)}, u32[]{:S(2)}) collective-permute-start(bf16[512,256]{1,0:T(8,128)(2,1)S(1)} %get-tuple-element.11), channel_id=1, source_target_pairs={{8,0},{16,8},{24,16},{32,24},{40,32},{48,40},{56,48},{64,56},{72,6... | collective-permute-start | bytes 786440 | tf_op jit(solution)/shard_map/ppermute | solution.py:18
  25.7 3.1 %copy-start.7 = (bf16[16,256,256]{2,1,0:T(8,128)(2,1)S(1)}, bf16[16,256,256]{2,1,0:T(8,128)(2,1)}, u32[]{:S(2)}) copy-start(bf16[16,256,256]{2,1,0:T(8,128)(2,1)} %gather_fusion) | copy-start | bytes 6291460
  28.8 2.5 %copy-start.5 = (bf16[16,256,256]{2,1,0:T(8,128)(2,1)S(1)}, bf16[16,256,256]{2,1,0:T(8,128)(2,1)}, u32[]{:S(2)}) copy-start(bf16[16,256,256]{2,1,0:T(8,128)(2,1)} %gather_fusion.1) | copy-start | bytes 6291460
  31.3 2.5 %copy-start.3 = (bf16[16,256,256]{2,1,0:T(8,128)(2,1)S(1)}, bf16[16,256,256]{2,1,0:T(8,128)(2,1)}, u32[]{:S(2)}) copy-start(bf16[16,256,256]{2,1,0:T(8,128)(2,1)} %gather_fusion.3) | copy-start | bytes 6291460
  31.3 5.5 %slice-start = ((s8[8388608]{0:T(1024)(128)(4,1)}), s8[4194304]{0:T(1024)(128)(4,1)S(1)}, s32[]{:S(2)}) async-start(s8[8388608]{0:T(1024)(128)(4,1)} %bitcast.81), calls=%async_computation.2 | async-start | bytes 8388608
  33.8 3.1 %slice-start.1 = ((s8[8388608]{0:T(1024)(128)(4,1)}), s8[4194304]{0:T(1024)(128)(4,1)S(1)}, s32[]{:S(2)}) async-start(s8[8388608]{0:T(1024)(128)(4,1)} %bitcast.81), calls=%async_computation.3 | async-start | bytes 8388608
  36.9 72.7 %copy-start.8 = (bf16[4096,256]{0,1:T(8,128)(2,1)S(1)}, bf16[4096,256]{0,1:T(8,128)(2,1)}, u32[]{:S(2)}) copy-start(bf16[4096,256]{0,1:T(8,128)(2,1)} %copy.30) | copy-start | bytes 6291460
  115.8 4.8 %copy-start = (bf16[4096,256]{0,1:T(8,128)(2,1)}, bf16[4096,256]{0,1:T(8,128)(2,1)S(1)}, u32[]{:S(2)}) copy-start(bf16[4096,256]{0,1:T(8,128)(2,1)S(1)} %get-tuple-element.17) | copy-start | bytes 6291460
  115.8 2.8 %collective-permute-start.2 = (bf16[512,256]{0,1:T(8,128)(2,1)S(1)}, bf16[512,256]{0,1:T(8,128)(2,1)S(1)}, u32[]{:S(2)}, u32[]{:S(2)}) collective-permute-start(bf16[512,256]{0,1:T(8,128)(2,1)S(1)} %get-tuple-element.8), channel_id=1, source_target_pairs={{0,8},{8,16},{16,24},{24,32},{32,40},{40,48},{48,56},{56,64},{64,7... | collective-permute-start | bytes 786440 | tf_op jit(solution)/shard_map/ppermute | solution.py:15
  117.2 3.4 %collective-permute-start.3 = (bf16[512,256]{0,1:T(8,128)(2,1)S(1)}, bf16[512,256]{0,1:T(8,128)(2,1)S(1)}, u32[]{:S(2)}, u32[]{:S(2)}) collective-permute-start(bf16[512,256]{0,1:T(8,128)(2,1)S(1)} %get-tuple-element.9), channel_id=1, source_target_pairs={{8,0},{16,8},{24,16},{32,24},{40,32},{48,40},{56,48},{64,56},{72,6... | collective-permute-start | bytes 786440 | tf_op jit(solution)/shard_map/ppermute | solution.py:18
  133.4 3.1 %copy-start.6 = (bf16[16,256,256]{2,1,0:T(8,128)(2,1)S(1)}, bf16[16,256,256]{2,1,0:T(8,128)(2,1)}, u32[]{:S(2)}) copy-start(bf16[16,256,256]{2,1,0:T(8,128)(2,1)} %gather_fusion.5) | copy-start | bytes 6291460
  136.5 2.5 %copy-start.4 = (bf16[16,256,256]{2,1,0:T(8,128)(2,1)S(1)}, bf16[16,256,256]{2,1,0:T(8,128)(2,1)}, u32[]{:S(2)}) copy-start(bf16[16,256,256]{2,1,0:T(8,128)(2,1)} %gather_fusion.6) | copy-start | bytes 6291460
  139.0 2.5 %copy-start.2 = (bf16[16,256,256]{2,1,0:T(8,128)(2,1)S(1)}, bf16[16,256,256]{2,1,0:T(8,128)(2,1)}, u32[]{:S(2)}) copy-start(bf16[16,256,256]{2,1,0:T(8,128)(2,1)} %gather_fusion.7) | copy-start | bytes 6291460
  139.0 5.5 %slice-start.2 = ((s8[8388608]{0:T(1024)(128)(4,1)}), s8[4194304]{0:T(1024)(128)(4,1)S(1)}, s32[]{:S(2)}) async-start(s8[8388608]{0:T(1024)(128)(4,1)} %bitcast.83), calls=%async_computation.4 | async-start | bytes 8388608
  141.5 3.1 %slice-start.3 = ((s8[8388608]{0:T(1024)(128)(4,1)}), s8[4194304]{0:T(1024)(128)(4,1)S(1)}, s32[]{:S(2)}) async-start(s8[8388608]{0:T(1024)(128)(4,1)} %bitcast.83), calls=%async_computation.5 | async-start | bytes 8388608
  146.9 2.0 copy-start.1
Sparse Core Ops, SparseCore 0:
  148.4 65.3 reduce-scatter.3
where the time goes:
time: 223 us; the launch traced here: 222 us
  blocking collectives  99.5 us (45%)
  waiting for transfers between devices  35.2 us (16%)
  matrix products  32.8 us (15%)
  local copies, waits for them, and re-layouts  30.6 us (14%)
  between operations  14.3 us (6%)
  starting transfers between devices  5.41 us (2%)
  other arithmetic  4.47 us (2%)
    psum x1, blocking collectives, on_device(): projection = lax.psum(partial_proj, 'basis')  70.3 us
    unnamed x2, waiting for transfers between devices  33.2 us
    psum x1, blocking collectives, on_device(): total_squares = lax.psum(squares, 'basis')  29.2 us
    dot_general x8, matrix products, band_local(): jnp.einsum('bij,bjc->bic', blocks[:, k], taken, preferred_element_type=jn...  21.9 us
    gather x8, local copies, waits for them, and re-layouts, band_local(): taken = stacked[index]  16.2 us
    unnamed x31, local copies, waits for them, and re-layouts  10.3 us
    dot_general x1, matrix products, on_device(): jnp.dot(target_orbitals, projection_b, preferred_element_type=jnp.float32)  6.21 us
  transfers between devices with their start and end apart: 5, of which 2 were waited for; matrix products, arithmetic and copies ran while one was open for 3% of the time, Pallas kernels for 0%

commit v1 on v0

--- a/solution.py
+++ b/solution.py
@@ -1,3 +1,4 @@
+import functools
 import jax
 import jax.numpy as jnp
 from jax import lax
@@ -5,6 +6,15 @@
 
 BK = 256
 KB = 4
+
+
+def _wrap_stops_all(w_in, net_axis):
+    next_value = jax.lax.all_gather(w_in, net_axis)
+    carry_out = jnp.sum(next_value, axis=0)
+    return carry_out
+
+
+number_orders = functools.partial(_wrap_stops_all, net_axis="basis")
 
 
 def padded_2(block, sides, width):
@@ -46,7 +56,7 @@
     cont_orth = (cont_orbitals.astype(jnp.float32) - removed).astype(jnp.bfloat16)
     squares = jnp.sum(jnp.square(cont_orth.astype(jnp.float32)), axis=0)
     orth_padded = padded_2(cont_orth, (("basis", 0),), 2 * BK)
-    total_squares = lax.psum(squares, "basis")
+    total_squares = number_orders(squares)
     col_norm = 1.0 / jnp.sqrt(
         total_squares / (band_offsets.shape[0] * BK * lax.axis_size("basis")) + 1e-06
     )

time: 223 us -> 223 us (level)
  blocking collectives: 99.5 us -> 90.4 us
  waiting for transfers between devices: 35.2 us -> 44.2 us
    psum x1 -> x0, blocking collectives: 29.2 us -> none  [on_device(): total_squares = lax.psum(squares, 'basis')]
    all_gather x0 -> x1, blocking collectives: none -> 20.1 us  [_wrap_stops_all(): next_value = jax.lax.all_gather(w_in, net_axis)]
    unnamed x2, waiting for transfers between devices: 33.2 us -> 42.3 us
where the time goes in v1:
time: 223 us; the launch traced here: 222 us
  blocking collectives  90.4 us (41%)
  waiting for transfers between devices  44.2 us (20%)
  matrix products  32.8 us (15%)
  local copies, waits for them, and re-layouts  30.6 us (14%)
  between operations  14.3 us (6%)
  starting transfers between devices  5.41 us (2%)
  other arithmetic  4.5 us (2%)
    psum x1, blocking collectives, on_device(): projection = lax.psum(partial_proj, 'basis')  70.3 us
    unnamed x2, waiting for transfers between devices  42.3 us
    dot_general x8, matrix products, band_local(): jnp.einsum('bij,bjc->bic', blocks[:, k], taken, preferred_element_type=jn...  21.9 us
    all_gather x1, blocking collectives, _wrap_stops_all(): next_value = jax.lax.all_gather(w_in, net_axis)  20.1 us
    gather x8, local copies, waits for them, and re-layouts, band_local(): taken = stacked[index]  16.2 us
    unnamed x31, local copies, waits for them, and re-layouts  10.3 us
    dot_general x1, matrix products, on_device(): jnp.dot(target_orbitals, projection_b, preferred_element_type=jnp.float32)  6.21 us
  transfers between devices with their start and end apart: 5, of which 2 were waited for; matrix products, arithmetic and copies ran while one was open for 3% of the time, Pallas kernels for 0%

profile of v1, /device:TPU:0, one launch (start us, length us, event | category | flops | bytes accessed | tf_op | source)
XLA Modules:
  0.0 222.3 jit_solution(400602679498883476)
XLA Ops:
  8.3 1.3 collective-permute-start
  11.7 4.1 %copy.30 = bf16[4096,256]{0,1:T(8,128)(2,1)} copy(bf16[4096,256]{1,0:T(8,128)(2,1)} %param.5) | data formatting | bytes 4194304 | tf_op args[0]
  15.9 1.8 pad_maximum_fusion
  17.6 2.0 gather_fusion.3
  19.6 2.0 gather_fusion.2
  21.6 2.0 gather_fusion.1
  23.7 2.0 gather_fusion
  25.7 3.1 %fusion.10 = f32[16,256,256]{1,2,0:T(8,128)S(1)} fusion(bf16[16,256,256]{2,1,0:T(8,128)(2,1)} %gather_fusion.2, bf16[16,4,256,256]{3,2,1,0:T(8,128)(2,1)} %param.7), kind=kOutput, calls=%fused_computation.24 | convolution fusion | flops 536870912 | bytes 8388608 | tf_op jit(solution)/shard_map/bij,bjc->bic/dot_general | solution.py:41
  28.8 2.5 %fusion.14 = f32[16,256,256]{1,2,0:T(8,128)S(1)} fusion(bf16[16,256,256]{2,1,0:T(8,128)(2,1)S(1)} %copy-done.7, bf16[16,4,256,256]{3,2,1,0:T(8,128)(2,1)} %param.7), kind=kOutput, calls=%fused_computation.28 | convolution fusion | flops 536870912 | bytes 8388608 | tf_op jit(solution)/shard_map/bij,bjc->bic/dot_general | solution.py:41
  31.3 2.5 %fusion.12 = f32[16,256,256]{1,2,0:T(8,128)S(1)} fusion(bf16[16,256,256]{2,1,0:T(8,128)(2,1)S(1)} %copy-done.5, bf16[16,4,256,256]{3,2,1,0:T(8,128)(2,1)} %param.7), kind=kOutput, calls=%fused_computation.26 | convolution fusion | flops 536870912 | bytes 8388608 | tf_op jit(solution)/shard_map/bij,bjc->bic/dot_general | solution.py:41
  33.8 3.0 %add_convert_fusion.1 = bf16[16,256,256]{1,2,0:T(8,128)(2,1)S(1)} fusion(f32[16,256,256]{1,2,0:T(8,128)S(1)} %fusion.10, f32[16,256,256]{1,2,0:T(8,128)S(1)} %fusion.14, f32[16,256,256]{1,2,0:T(8,128)S(1)} %fusion.12, bf16[16,256,256]{2,1,0:T(8,128)(2,1)S(1)} %copy-done.3, bf16[16,4,256,256]{3,2,1,0:T(8,128)(2,1)} %param.7), kind=kOutput, calls=%fused_computation.13 | convolution fusion | flops 541065216 | bytes 18874368 | tf_op jit(solution)/shard_map/bij,bjc->bic/dot_general | solution.py:41
  36.9 2.3 %convolution_bitcast_fusion.2 = f32[1024,256]{0,1:T(8,128)S(1)} fusion(bf16[4096,256]{1,0:T(8,128)(2,1)S(1)} %bitcast.94, bf16[4096,1024]{1,0:T(8,128)(2,1)S(1)} %bitcast.83), kind=kOutput, calls=%fused_computation.39 | convolution fusion | flops 2147483648 | bytes 11534336 | tf_op jit(solution)/shard_map/dot_general | solution.py:50
  39.2 70.3 %all-reduce.1 = bf16[1024,256]{0,1:T(8,128)(2,1)} all-reduce(f32[1024,256]{0,1:T(8,128)S(1)} %convolution_bitcast_fusion.2), channel_id=1, replica_groups=mesh['basis'=16,'orb'=8] {'basis'}, use_global_device_ids=true, to_apply=%region_0.0 | all-reduce | flops 262144 | bytes 1572864 | tf_op jit(solution)/shard_map/psum | solution.py:53
  109.6 6.2 %multiply_reduce_fusion = (f32[256]{0:T(256)S(1)}, bf16[4096,256]{0,1:T(8,128)(2,1)S(1)}) fusion(bf16[1024,256]{0,1:T(8,128)(2,1)} %all-reduce.1, bf16[4096,1024]{1,0:T(8,128)(2,1)} %param.6, bf16[4096,256]{0,1:T(8,128)(2,1)S(1)} %copy-done.8), kind=kOutput, calls=%fused_computation.11 | convolution fusion | flops 2153774848 | bytes 13108224 | tf_op jit(solution)/shard_map/dot_general | solution.py:55
  115.8 1.3 collective-permute-start.2
  117.2 1.5 collective-permute-start.3
  118.6 1.9 collective-permute-done.3
  120.6 1.7 pad_maximum_fusion.1
  122.3 3.0 %copy.35 = bf16[5120,256]{1,0:T(8,128)(2,1)S(1)} copy(bf16[5120,256]{0,1:T(8,128)(2,1)} %pad_maximum_fusion.1) | data formatting | bytes 5242880 | tf_op jit(solution)/shard_map/concatenate | solution.py:29
  125.3 2.0 gather_fusion.7
  127.3 2.0 gather_fusion.6
  129.3 2.0 gather_fusion.5
  131.4 2.0 gather_fusion.4
  133.4 3.1 %fusion.7 = f32[16,256,256]{1,2,0:T(8,128)S(1)} fusion(bf16[16,256,256]{2,1,0:T(8,128)(2,1)} %gather_fusion.4, bf16[16,4,256,256]{3,2,1,0:T(8,128)(2,1)} %param.8), kind=kOutput, calls=%fused_computation.21 | convolution fusion | flops 536870912 | bytes 8388608 | tf_op jit(solution)/shard_map/bij,bjc->bic/dot_general | solution.py:41
  136.5 2.5 %fusion.5 = f32[16,256,256]{1,2,0:T(8,128)S(1)} fusion(bf16[16,256,256]{2,1,0:T(8,128)(2,1)S(1)} %copy-done.6, bf16[16,4,256,256]{3,2,1,0:T(8,128)(2,1)} %param.8), kind=kOutput, calls=%fused_computation.19 | convolution fusion | flops 536870912 | bytes 8388608 | tf_op jit(solution)/shard_map/bij,bjc->bic/dot_general | solution.py:41
  139.0 2.5 %fusion.3 = f32[16,256,256]{1,2,0:T(8,128)S(1)} fusion(bf16[16,256,256]{2,1,0:T(8,128)(2,1)S(1)} %copy-done.4, bf16[16,4,256,256]{3,2,1,0:T(8,128)(2,1)} %param.8), kind=kOutput, calls=%fused_computation.17 | convolution fusion | flops 536870912 | bytes 8388608 | tf_op jit(solution)/shard_map/bij,bjc->bic/dot_general | solution.py:41
  141.5 3.0 %add_convert_fusion = bf16[16,256,256]{1,2,0:T(8,128)(2,1)S(1)} fusion(f32[16,256,256]{1,2,0:T(8,128)S(1)} %fusion.3, f32[16,256,256]{1,2,0:T(8,128)S(1)} %fusion.7, f32[16,256,256]{1,2,0:T(8,128)S(1)} %fusion.5, bf16[16,256,256]{2,1,0:T(8,128)(2,1)S(1)} %copy-done.2, bf16[16,4,256,256]{3,2,1,0:T(8,128)(2,1)} %param.8), kind=kOutput, calls=%fused_computation.12 | convolution fusion | flops 541065216 | bytes 18874368 | tf_op jit(solution)/shard_map/bij,bjc->bic/dot_general | solution.py:41
  144.6 2.3 %convolution_bitcast_fusion.1 = f32[1024,256]{0,1:T(8,128)S(1)} fusion(bf16[4096,256]{1,0:T(8,128)(2,1)S(1)} %bitcast.95, bf16[4096,1024]{1,0:T(8,128)(2,1)S(1)} %bitcast.85), kind=kOutput, calls=%fused_computation.38 | convolution fusion | flops 2147483648 | bytes 11534336 | tf_op jit(solution)/shard_map/dot_general | solution.py:65
  146.9 1.3 copy.42
  148.9 2.4 %copy.40 = bf16[4096,256]{1,0:T(8,128)(2,1)} copy(bf16[4096,256]{0,1:T(8,128)(2,1)S(1)} %copy-done.1) | data formatting | bytes 4194304
  151.3 20.1 %all-gather.1 = f32[16,1,256]{2,1,0:T(1,128)S(1)} all-gather(f32[1,1,256]{2,1,0:T(1,128)S(1)} %bitcast.96), channel_id=2, replica_groups=mesh['basis'=16,'orb'=8] {'basis'}, dimensions={0}, use_global_device_ids=true | all-gather | bytes 17408 | tf_op jit(solution)/shard_map/all_gather | solution.py:12
  171.5 42.3 %reduce-scatter.4.cloned.1.call-done = f32[64,256]{1,0:T(8,128)} async-done(((f32[1024,256]{1,0:T(8,128)}), f32[64,256]{1,0:T(8,128)}) %reduce-scatter.4.cloned.1.call-update) | async-done | bytes 65552
  (44 shorter events, 5.9 us)
Async XLA Ops:
  7.2 206.6 %reduce-scatter.4.cloned.1.call-start = ((), (), s32[]{:S(2)}) async-start(), calls=%async_computation.1 | async-start | bytes 1114112
  8.3 7.6 %collective-permute-start = (bf16[512,256]{1,0:T(8,128)(2,1)S(1)}, bf16[512,256]{1,0:T(8,128)(2,1)S(1)}, u32[]{:S(2)}, u32[]{:S(2)}) collective-permute-start(bf16[512,256]{1,0:T(8,128)(2,1)S(1)} %get-tuple-element.10), channel_id=1, source_target_pairs={{0,8},{8,16},{16,24},{24,32},{32,40},{40,48},{48,56},{56,64},{64,7... | collective-permute-start | bytes 786440 | tf_op jit(solution)/shard_map/ppermute | solution.py:25
  9.6 6.3 %collective-permute-start.1 = (bf16[512,256]{1,0:T(8,128)(2,1)S(1)}, bf16[512,256]{1,0:T(8,128)(2,1)S(1)}, u32[]{:S(2)}, u32[]{:S(2)}) collective-permute-start(bf16[512,256]{1,0:T(8,128)(2,1)S(1)} %get-tuple-element.11), channel_id=1, source_target_pairs={{8,0},{16,8},{24,16},{32,24},{40,32},{48,40},{56,48},{64,56},{72,6... | collective-permute-start | bytes 786440 | tf_op jit(solution)/shard_map/ppermute | solution.py:28
  25.7 3.1 %copy-start.7 = (bf16[16,256,256]{2,1,0:T(8,128)(2,1)S(1)}, bf16[16,256,256]{2,1,0:T(8,128)(2,1)}, u32[]{:S(2)}) copy-start(bf16[16,256,256]{2,1,0:T(8,128)(2,1)} %gather_fusion) | copy-start | bytes 6291460
  28.8 2.5 %copy-start.5 = (bf16[16,256,256]{2,1,0:T(8,128)(2,1)S(1)}, bf16[16,256,256]{2,1,0:T(8,128)(2,1)}, u32[]{:S(2)}) copy-start(bf16[16,256,256]{2,1,0:T(8,128)(2,1)} %gather_fusion.1) | copy-start | bytes 6291460
  31.3 2.5 %copy-start.3 = (bf16[16,256,256]{2,1,0:T(8,128)(2,1)S(1)}, bf16[16,256,256]{2,1,0:T(8,128)(2,1)}, u32[]{:S(2)}) copy-start(bf16[16,256,256]{2,1,0:T(8,128)(2,1)} %gather_fusion.3) | copy-start | bytes 6291460
  31.3 5.5 %slice-start = ((s8[8388608]{0:T(1024)(128)(4,1)}), s8[4194304]{0:T(1024)(128)(4,1)S(1)}, s32[]{:S(2)}) async-start(s8[8388608]{0:T(1024)(128)(4,1)} %bitcast.82), calls=%async_computation.2 | async-start | bytes 8388608
  33.8 3.1 %slice-start.1 = ((s8[8388608]{0:T(1024)(128)(4,1)}), s8[4194304]{0:T(1024)(128)(4,1)S(1)}, s32[]{:S(2)}) async-start(s8[8388608]{0:T(1024)(128)(4,1)} %bitcast.82), calls=%async_computation.3 | async-start | bytes 8388608
  36.9 72.7 %copy-start.8 = (bf16[4096,256]{0,1:T(8,128)(2,1)S(1)}, bf16[4096,256]{0,1:T(8,128)(2,1)}, u32[]{:S(2)}) copy-start(bf16[4096,256]{0,1:T(8,128)(2,1)} %copy.30) | copy-start | bytes 6291460
  115.8 4.8 %copy-start = (bf16[4096,256]{0,1:T(8,128)(2,1)}, bf16[4096,256]{0,1:T(8,128)(2,1)S(1)}, u32[]{:S(2)}) copy-start(bf16[4096,256]{0,1:T(8,128)(2,1)S(1)} %get-tuple-element.17) | copy-start | bytes 6291460
  115.8 2.8 %collective-permute-start.2 = (bf16[512,256]{0,1:T(8,128)(2,1)S(1)}, bf16[512,256]{0,1:T(8,128)(2,1)S(1)}, u32[]{:S(2)}, u32[]{:S(2)}) collective-permute-start(bf16[512,256]{0,1:T(8,128)(2,1)S(1)} %get-tuple-element.8), channel_id=1, source_target_pairs={{0,8},{8,16},{16,24},{24,32},{32,40},{40,48},{48,56},{56,64},{64,7... | collective-permute-start | bytes 786440 | tf_op jit(solution)/shard_map/ppermute | solution.py:25
  117.2 3.4 %collective-permute-start.3 = (bf16[512,256]{0,1:T(8,128)(2,1)S(1)}, bf16[512,256]{0,1:T(8,128)(2,1)S(1)}, u32[]{:S(2)}, u32[]{:S(2)}) collective-permute-start(bf16[512,256]{0,1:T(8,128)(2,1)S(1)} %get-tuple-element.9), channel_id=1, source_target_pairs={{8,0},{16,8},{24,16},{32,24},{40,32},{48,40},{56,48},{64,56},{72,6... | collective-permute-start | bytes 786440 | tf_op jit(solution)/shard_map/ppermute | solution.py:28
  133.4 3.1 %copy-start.6 = (bf16[16,256,256]{2,1,0:T(8,128)(2,1)S(1)}, bf16[16,256,256]{2,1,0:T(8,128)(2,1)}, u32[]{:S(2)}) copy-start(bf16[16,256,256]{2,1,0:T(8,128)(2,1)} %gather_fusion.5) | copy-start | bytes 6291460
  136.5 2.5 %copy-start.4 = (bf16[16,256,256]{2,1,0:T(8,128)(2,1)S(1)}, bf16[16,256,256]{2,1,0:T(8,128)(2,1)}, u32[]{:S(2)}) copy-start(bf16[16,256,256]{2,1,0:T(8,128)(2,1)} %gather_fusion.6) | copy-start | bytes 6291460
  139.0 2.5 %copy-start.2 = (bf16[16,256,256]{2,1,0:T(8,128)(2,1)S(1)}, bf16[16,256,256]{2,1,0:T(8,128)(2,1)}, u32[]{:S(2)}) copy-start(bf16[16,256,256]{2,1,0:T(8,128)(2,1)} %gather_fusion.7) | copy-start | bytes 6291460
  139.0 5.5 %slice-start.2 = ((s8[8388608]{0:T(1024)(128)(4,1)}), s8[4194304]{0:T(1024)(128)(4,1)S(1)}, s32[]{:S(2)}) async-start(s8[8388608]{0:T(1024)(128)(4,1)} %bitcast.84), calls=%async_computation.4 | async-start | bytes 8388608
  141.5 3.1 %slice-start.3 = ((s8[8388608]{0:T(1024)(128)(4,1)}), s8[4194304]{0:T(1024)(128)(4,1)S(1)}, s32[]{:S(2)}) async-start(s8[8388608]{0:T(1024)(128)(4,1)} %bitcast.84), calls=%async_computation.5 | async-start | bytes 8388608
  146.9 2.0 copy-start.1
Sparse Core Ops, SparseCore 0:
  148.4 65.2 reduce-scatter.3
